TPU v7x, 128 devices: a whole 4x4x4 slice. The times are simulated.
128 devices in a mesh: sens: 8 (over x, y_hi), par: 16 (over y_lo, z, core).
Axes of the slice: x: 4, y: 4 (y_hi: 2, y_lo: 2; y = y_hi * 2 + y_lo), z: 4, core: 2. Of those that a mesh axis runs over, the one named last changes fastest.
Arguments:
- records: float32 [16, 600, 224], P(None, 'sens'), may hold values from -6 to 6
- spec_real: float32 [225, 600, 2048], P(None, 'sens', 'par'), may hold values from -0.109375 to 0.109375
- spec_imag: float32 [225, 600, 2048], P(None, 'sens', 'par'), may hold values from -0.109375 to 0.109375
- prior_cov: float32 [224, 224], replicated, as said below
- sensor_map: int32 [600], replicated, may hold values from 0 to 599, each once
- inverse_rows: float32 [768, 224, 600], P('sens', 'par'), may hold values from -0.015625 to 0.015625
Outputs:
- update: float32 [16, 768], P('par', 'sens')
Inputs may be any that keep to these rules, and one draw needn't show every extreme that they name: prior_cov is symmetric. sensor_map names every sensor once.
All inputs are finite; a program needn't handle non-finite values.
Results may differ from a plain program's by a relative error of at most 0.00013.
Values sent between devices are 32-bit elements; how exact they have to be, the bound alone decides.
A program may use at most 128 MiB of HBM per device.

v0:
```python
import math

import jax
import jax.numpy as jnp
from jax import lax
from jax.sharding import PartitionSpec as P

highest = lax.Precision.HIGHEST


def cut_along(x, dim, length):
    before, after = (x.shape[:dim], x.shape[dim + 1 :])
    return jnp.moveaxis(x.reshape(*before, length, -1, *after), dim, 0)


def sum_at_owner(x, axis, dim):
    pieces = cut_along(x, dim, lax.axis_size(axis))
    arrived = lax.all_to_all(pieces, axis, split_axis=0, concat_axis=0, tiled=True)
    return arrived.sum(axis=0)


def side_by_side(arrays, axis, dim, along):
    ends, at = ([], 0)
    for a in arrays[:-1]:
        at += a.shape[along]
        ends.append(at)
    both = jnp.concatenate(arrays, axis=along)
    return tuple(jnp.split(lax.all_gather(both, axis, axis=dim, tiled=True), ends, axis=along))


def laid_out(pieces, dim):
    pieces = jnp.moveaxis(pieces, 0, dim)
    lengths = pieces.shape
    return pieces.reshape(*lengths[:dim], lengths[dim] * lengths[dim + 1], *lengths[dim + 2 :])


def from_everyone(x, axis):
    copies = jnp.broadcast_to(x, (lax.axis_size(axis), *x.shape))
    return lax.all_to_all(copies, axis, split_axis=0, concat_axis=0, tiled=True)


def gathered_copies(x, axis, dim):
    return laid_out(from_everyone(x, axis), dim)


def spectrum_tables(num_steps, length):
    sample = jnp.arange(num_steps, dtype=jnp.int32)[:, None]
    frequency = jnp.arange(num_steps + 1, dtype=jnp.int32)[None, :]
    phases = (sample * frequency % length).astype(jnp.float32) * (2.0 * math.pi / length)
    return (jnp.cos(phases), -jnp.sin(phases))


def inverse_tables(sample_index, num_steps, length):
    frequency = jnp.arange(num_steps + 1, dtype=jnp.int32)[:, None]
    phases = (frequency * sample_index[None, :] % length).astype(jnp.float32) * (
        2.0 * math.pi / length
    )
    edge_bins = (frequency == 0) | (frequency == num_steps)
    weights = jnp.where(edge_bins, 1.0, 2.0).astype(jnp.float32) / length
    return (weights * jnp.cos(phases), -weights * jnp.sin(phases))


def to_spectrum(signal, cosine, minus_sine):
    part_real = jnp.dot(signal, cosine, precision=highest, preferred_element_type=jnp.float32)
    part_imag = jnp.dot(signal, minus_sine, precision=highest, preferred_element_type=jnp.float32)
    return (part_real, part_imag)


def to_times(part_real, part_imag, cosine, minus_sine):
    first_term = jnp.dot(part_real, cosine, precision=highest, preferred_element_type=jnp.float32)
    return first_term + jnp.dot(
        part_imag, minus_sine, precision=highest, preferred_element_type=jnp.float32
    )


def shards(records, spec_real, spec_imag, prior_cov, sensor_map, inverse_rows):
    num_steps = records.shape[2]
    length = 2 * num_steps
    cols_all = records.shape[0]
    sens_dev = spec_real.shape[1]
    block_steps = num_steps // lax.axis_size("par")
    fwd_cos, fwd_sin = spectrum_tables(num_steps, length)
    inv_cos, inv_sin = inverse_tables(jnp.arange(num_steps, dtype=jnp.int32), num_steps, length)
    prior_cos = jnp.dot(prior_cov, fwd_cos, precision=highest, preferred_element_type=jnp.float32)
    prior_sin = jnp.dot(prior_cov, fwd_sin, precision=highest, preferred_element_type=jnp.float32)
    rec_real, rec_imag = to_spectrum(records, fwd_cos, fwd_sin)
    adj_real = jnp.einsum(
        "csw,wsp->cpw", rec_real, spec_real, precision=highest, preferred_element_type=jnp.float32
    )
    adj_real = adj_real + jnp.einsum(
        "csw,wsp->cpw", rec_imag, spec_imag, precision=highest, preferred_element_type=jnp.float32
    )
    adj_imag = jnp.einsum(
        "csw,wsp->cpw", rec_imag, spec_real, precision=highest, preferred_element_type=jnp.float32
    )
    adj_imag = adj_imag - jnp.einsum(
        "csw,wsp->cpw", rec_real, spec_imag, precision=highest, preferred_element_type=jnp.float32
    )
    partial_adj = to_times(adj_real, adj_imag, inv_cos, inv_sin)
    share_cols = sum_at_owner(partial_adj, "sens", 0)
    share_real, share_imag = to_spectrum(share_cols, prior_cos, prior_sin)
    field_real, field_imag = side_by_side((share_real, share_imag), "sens", 0, 1)
    pred_real = jnp.einsum(
        "cpw,wsp->csw", field_real, spec_real, precision=highest, preferred_element_type=jnp.float32
    )
    pred_real = pred_real - jnp.einsum(
        "cpw,wsp->csw", field_imag, spec_imag, precision=highest, preferred_element_type=jnp.float32
    )
    pred_imag = jnp.einsum(
        "cpw,wsp->csw", field_imag, spec_real, precision=highest, preferred_element_type=jnp.float32
    )
    pred_imag = pred_imag + jnp.einsum(
        "cpw,wsp->csw", field_real, spec_imag, precision=highest, preferred_element_type=jnp.float32
    )
    partial_pred = jnp.einsum(
        "csw,wt->cts", pred_real, inv_cos, precision=highest, preferred_element_type=jnp.float32
    )
    partial_pred = partial_pred + jnp.einsum(
        "csw,wt->cts", pred_imag, inv_sin, precision=highest, preferred_element_type=jnp.float32
    )
    partial_flat = partial_pred.reshape(cols_all, num_steps * sens_dev)
    predicted = sum_at_owner(partial_flat, "par", 1)
    gathered = gathered_copies(predicted, "sens", 1)
    step_index = jnp.arange(block_steps, dtype=jnp.int32)[:, None]
    pick_index = (
        (sensor_map // sens_dev)[None, :] * (block_steps * sens_dev)
        + step_index * sens_dev
        + (sensor_map % sens_dev)[None, :]
    )
    permuted = jnp.take(gathered, pick_index, axis=1)
    flat_data = permuted.reshape(cols_all, -1)
    flat_rows = inverse_rows.reshape(inverse_rows.shape[0], -1)
    partial_update = jnp.einsum(
        "ck,rk->cr", flat_data, flat_rows, precision=highest, preferred_element_type=jnp.float32
    )
    return sum_at_owner(partial_update, "par", 0)


def solution(mesh):
    return jax.shard_map(
        shards,
        mesh=mesh,
        in_specs=(
            P(None, "sens", None),
            P(None, "sens", "par"),
            P(None, "sens", "par"),
            P(),
            P(),
            P("sens", "par", None),
        ),
        out_specs=P("par", "sens"),
        check_vma=False,
    )
```

profile of v0, /device:TPU:1, one launch (start us, length us, event | category | flops | bytes accessed | tf_op | source)
XLA Modules:
  0.0 362.2 jit_solution(3370160515814636957)
XLA Ops:
  6.5 5.1 %convolution_bitcast_fusion.1 = f32[16,75,225]{2,1,0:T(8,128)} fusion(f32[16,75,224]{2,0,1:T(8,128)} %param.6), kind=kOutput, calls=%fused_computation.35 | convolution fusion | flops 726213632 | bytes 2155200 | tf_op jit(solution)/shard_map/dot_general | solution.py:64
  11.6 3.7 %convolution_bitcast_fusion = f32[16,75,225]{2,1,0:T(8,128)} fusion(f32[16,75,224]{2,0,1:T(8,128)S(1)} %copy-done.3), kind=kOutput, calls=%fused_computation.34 | convolution fusion | flops 726264000 | bytes 2155200 | tf_op jit(solution)/shard_map/dot_general | solution.py:65
  15.3 3.1 copy.16
  18.4 2.8 copy.19
  21.3 13.4 %fusion.4 = f32[225,16,128]{2,1,0:T(8,128)S(1)} fusion(f32[16,75,225]{1,0,2:T(8,128)} %copy.16, f32[225,75,128]{2,0,1:T(8,128)} %param.8), kind=kOutput, calls=%fused_computation.5 | convolution fusion | flops 414720000 | bytes 11563200 | tf_op jit(solution)/shard_map/csw,wsp->cpw/dot_general | solution.py:96
  34.7 13.6 %fusion.6 = f32[225,16,128]{2,1,0:T(8,128)S(1)} fusion(f32[16,75,225]{1,0,2:T(8,128)S(1)} %copy-done.2, f32[225,75,128]{2,0,1:T(8,128)} %param.8), kind=kOutput, calls=%fused_computation.7 | convolution fusion | flops 414720000 | bytes 11563200 | tf_op jit(solution)/shard_map/csw,wsp->cpw/dot_general | solution.py:90
  48.3 8.8 %subtract_bitcast_fusion.1 = f32[16,128,225]{1,0,2:T(8,128)S(1)} fusion(f32[225,16,128]{2,1,0:T(8,128)S(1)} %fusion.4, f32[16,75,225]{1,0,2:T(8,128)S(1)} %copy-done.2, f32[225,75,128]{2,0,1:T(8,128)S(1)} %bitcast.60), kind=kOutput, calls=%fused_computation.27 | convolution fusion | flops 415180800 | bytes 13406400 | tf_op jit(solution)/shard_map/csw,wsp->cpw/dot_general | solution.py:93
  57.1 8.9 %add_bitcast_fusion.1 = f32[16,128,225]{1,0,2:T(8,128)S(1)} fusion(f32[225,16,128]{2,1,0:T(8,128)S(1)} %fusion.6, f32[16,75,225]{1,0,2:T(8,128)S(1)} %copy-done.1, f32[225,75,128]{2,0,1:T(8,128)S(1)} %bitcast.60), kind=kOutput, calls=%fused_computation.28 | convolution fusion | flops 415180800 | bytes 13406400 | tf_op jit(solution)/shard_map/csw,wsp->cpw/dot_general | solution.py:87
  66.0 3.0 fusion.20
  69.0 4.3 %fusion.40 = f32[16,128,224]{1,2,0:T(8,128)} fusion(f32[16,128,224]{1,2,0:T(8,128)S(1)} %fusion.20, f32[16,128,225]{1,0,2:T(8,128)S(1)} %add_bitcast_fusion.1, f32[225]{0:T(256)S(1)} %fusion.108), kind=kOutput, calls=%fused_computation.33 | convolution fusion | flops 1239593216 | bytes 5514116 | tf_op jit(solution)/shard_map/dot_general | solution.py:70
  73.3 7.5 %all-to-all-start = ((f32[8,2,128,224]{2,3,1,0:T(8,128)}), f32[8,2,128,224]{2,3,1,0:T(8,128)}, u32[]{:S(2)}, u32[]{:S(2)}) async-start(f32[8,2,128,224]{2,3,1,0:T(8,128)} %bitcast.63), calls=%async_computation | async-start | bytes 3670016 | tf_op jit(solution)/shard_map/all_to_all | solution.py:18
  81.2 2.9 convolution_bitcast_fusion.3
  84.1 2.9 convolution_bitcast_fusion.2
  87.0 20.6 %all-to-all-done = f32[8,2,128,224]{2,3,1,0:T(8,128)} async-done(((f32[8,2,128,224]{2,3,1,0:T(8,128)}), f32[8,2,128,224]{2,3,1,0:T(8,128)}, u32[]{:S(2)}, u32[]{:S(2)}) %all-to-all-start) | async-done | bytes 1835040 | tf_op jit(solution)/shard_map/all_to_all | solution.py:18
  114.1 67.0 %all-gather.2.cloned.1.call-done = f32[16,256,225]{1,2,0:T(8,128)} async-done(((f32[2,256,225]{1,2,0:T(8,128)}), f32[16,256,225]{1,2,0:T(8,128)}) %all-gather.2.cloned.1.call-update) | async-done | bytes 3686416 | tf_op jit(solution)/shard_map/all_gather | solution.py:28
  183.5 19.5 %fusion = f32[225,16,75]{2,1,0:T(8,128)S(1)} fusion(f32[225,75,128]{2,0,1:T(8,128)} %param.8, f32[16,128,225]{1,2,0:T(8,128)S(1)} %get-tuple-element.6), kind=kOutput, calls=%fused_computation.1 | convolution fusion | flops 414720000 | bytes 11563200 | tf_op jit(solution)/shard_map/cpw,wsp->csw/dot_general | solution.py:112
  203.0 19.5 %fusion.2 = f32[225,16,75]{2,1,0:T(8,128)S(1)} fusion(f32[225,75,128]{2,0,1:T(8,128)} %param.8, f32[16,128,225]{1,2,0:T(8,128)S(1)} %get-tuple-element.5), kind=kOutput, calls=%fused_computation.3 | convolution fusion | flops 414720000 | bytes 11563200 | tf_op jit(solution)/shard_map/cpw,wsp->csw/dot_general | solution.py:106
  222.6 14.4 %add_bitcast_fusion = f32[16,75,225]{1,0,2:T(8,128)S(1)} fusion(f32[225,16,75]{2,1,0:T(8,128)S(1)} %fusion, f32[225,75,128]{2,0,1:T(8,128)S(1)} %bitcast.62, f32[16,128,225]{1,2,0:T(8,128)S(1)} %get-tuple-element.5), kind=kOutput, calls=%fused_computation.25 | convolution fusion | flops 414990016 | bytes 12643200 | tf_op jit(solution)/shard_map/cpw,wsp->csw/dot_general | solution.py:109
  237.0 4.4 %fusion.16 = f32[224,16,75]{0,2,1:T(8,128)S(1)} fusion(f32[16,75,225]{1,0,2:T(8,128)S(1)} %add_bitcast_fusion, f32[225]{0:T(256)S(1)} %fusion.109), kind=kOutput, calls=%fused_computation.17 | convolution fusion | flops 726264000 | bytes 2156100 | tf_op jit(solution)/shard_map/csw,wt->cts/dot_general | solution.py:118
  241.4 14.8 %subtract_bitcast_fusion = f32[16,75,225]{1,0,2:T(8,128)S(1)} fusion(f32[225,16,75]{2,1,0:T(8,128)S(1)} %fusion.2, f32[225,75,128]{2,0,1:T(8,128)S(1)} %bitcast.62, f32[16,128,225]{1,2,0:T(8,128)S(1)} %get-tuple-element.6), kind=kOutput, calls=%fused_computation.26 | convolution fusion | flops 414990016 | bytes 12643200 | tf_op jit(solution)/shard_map/cpw,wsp->csw/dot_general | solution.py:103
  256.1 5.2 %fusion.46 = f32[16,224,75]{1,2,0:T(8,128)} fusion(f32[224,16,75]{0,2,1:T(8,128)S(1)} %fusion.16, f32[16,75,225]{1,0,2:T(8,128)S(1)} %subtract_bitcast_fusion, f32[225]{0:T(256)S(1)} %fusion.108), kind=kOutput, calls=%fused_computation.37 | convolution fusion | flops 726532800 | bytes 3231300 | tf_op jit(solution)/shard_map/csw,wt->cts/dot_general | solution.py:115
  261.4 3.2 copy.35
  264.5 2.8 reshape_reshape.3
  270.0 5.9 %all-to-all-start.1 = ((f32[16,16,1050]{2,1,0:T(8,128)}), f32[16,16,1050]{2,1,0:T(8,128)}, u32[]{:S(2)}, u32[]{:S(2)}) async-start(f32[16,16,1050]{2,1,0:T(8,128)} %copy.36), calls=%async_computation.1 | async-start | bytes 2359296 | tf_op jit(solution)/shard_map/all_to_all | solution.py:18
  275.9 17.2 %all-to-all-done.1 = f32[16,16,1050]{2,1,0:T(8,128)} async-done(((f32[16,16,1050]{2,1,0:T(8,128)}), f32[16,16,1050]{2,1,0:T(8,128)}, u32[]{:S(2)}, u32[]{:S(2)}) %all-to-all-start.1) | async-done | bytes 1075232 | tf_op jit(solution)/shard_map/all_to_all | solution.py:18
  295.3 4.4 %all-to-all-start.2 = ((f32[8,16,1050]{2,1,0:T(8,128)}), f32[8,16,1050]{2,1,0:T(8,128)}, u32[]{:S(2)}, u32[]{:S(2)}) async-start(f32[8,16,1050]{2,1,0:T(8,128)} %broadcast_in_dim.31), calls=%async_computation.2 | async-start | bytes 1179648 | tf_op jit(solution)/shard_map/all_to_all | solution.py:39
  300.0 10.8 %all-to-all-done.2 = f32[8,16,1050]{2,1,0:T(8,128)} async-done(((f32[8,16,1050]{2,1,0:T(8,128)}), f32[8,16,1050]{2,1,0:T(8,128)}, u32[]{:S(2)}, u32[]{:S(2)}) %all-to-all-start.2) | async-done | bytes 537632 | tf_op jit(solution)/shard_map/all_to_all | solution.py:39
  314.9 3.6 copy.38
  318.5 18.6 %gather_fusion = f32[8400,16]{1,0:T(8,128)} fusion(f32[16,8400]{0,1:T(8,128)} %copy.38, s32[9216]{0:T(1024)S(1)} %pad_clamp_fusion), kind=kCustom, calls=%fused_computation | custom fusion | bytes 1108800 | tf_op jit(solution)/shard_map/jit(_take)/gather | solution.py:130
  337.1 3.6 copy.39
  340.7 3.8 %fusion.51 = f32[16,96,1]{1,0,2:T(8,128)S(1)} fusion(f32[96,14,600]{2,0,1:T(8,128)S(1)} %copy-done, f32[14,600,16]{1,2,0:T(8,128)} %copy.39, pred[14,600]{1,0:T(8,128)(4,1)S(1)} %fusion.105), kind=kOutput, calls=%fused_computation.42 | convolution fusion | flops 154963200 | bytes 3777744 | tf_op jit(solution)/shard_map/ck,rk->cr/dot_general | solution.py:133
  344.5 10.1 %all_to_all.20 = f32[16,1,96]{2,1,0:T(1,128)S(1)} all-to-all(f32[16,1,96]{2,1,0:T(1,128)S(1)} %bitcast.66), channel_id=1, replica_groups=mesh['sens'=8,'par'=16] {'par'}, dimensions={0} | all-to-all | bytes 12288 | tf_op jit(solution)/shard_map/all_to_all | solution.py:18
  (45 shorter events, 19.2 us)
Async XLA Ops:
  6.5 334.2 %copy-start = (f32[96,14,600]{2,0,1:T(8,128)S(1)}, f32[96,14,600]{2,0,1:T(8,128)}, u32[]{:S(2)}) copy-start(f32[96,14,600]{2,0,1:T(8,128)} %param.11) | copy-start | bytes 9676804
  6.5 5.1 %copy-start.3 = (f32[16,75,224]{2,0,1:T(8,128)S(1)}, f32[16,75,224]{2,0,1:T(8,128)}, u32[]{:S(2)}) copy-start(f32[16,75,224]{2,0,1:T(8,128)} %param.6) | copy-start | bytes 3225604
  21.2 13.4 %copy-start.2 = (f32[16,75,225]{1,0,2:T(8,128)S(1)}, f32[16,75,225]{1,0,2:T(8,128)}, u32[]{:S(2)}) copy-start(f32[16,75,225]{1,0,2:T(8,128)} %copy.19) | copy-start | bytes 3240004
  21.2 27.0 %slice-start = ((s8[8908800]{0:T(1024)(128)(4,1)}), s8[4194304]{0:T(1024)(128)(4,1)S(1)}, s32[]{:S(2)}) async-start(s8[8908800]{0:T(1024)(128)(4,1)} %bitcast.59), calls=%async_computation.5 | async-start | bytes 8388608
  21.3 27.0 %slice-start.1 = ((s8[8908800]{0:T(1024)(128)(4,1)}), s8[4194304]{0:T(1024)(128)(4,1)S(1)}, s32[]{:S(2)}) async-start(s8[8908800]{0:T(1024)(128)(4,1)} %bitcast.59), calls=%async_computation.6 | async-start | bytes 8388608
  34.7 13.6 %slice-start.2 = ((s8[8908800]{0:T(1024)(128)(4,1)}), s8[520192]{0:T(1024)(128)(4,1)S(1)}, s32[]{:S(2)}) async-start(s8[8908800]{0:T(1024)(128)(4,1)} %bitcast.59), calls=%async_computation.7 | async-start | bytes 1040384
  48.3 8.8 %copy-start.1 = (f32[16,75,225]{1,0,2:T(8,128)S(1)}, f32[16,75,225]{1,0,2:T(8,128)}, u32[]{:S(2)}) copy-start(f32[16,75,225]{1,0,2:T(8,128)} %copy.16) | copy-start | bytes 3240004
  73.3 34.4 %all-to-all-start = ((f32[8,2,128,224]{2,3,1,0:T(8,128)}), f32[8,2,128,224]{2,3,1,0:T(8,128)}, u32[]{:S(2)}, u32[]{:S(2)}) async-start(f32[8,2,128,224]{2,3,1,0:T(8,128)} %bitcast.63), calls=%async_computation | async-start | bytes 3670016 | tf_op jit(solution)/shard_map/all_to_all | solution.py:18
  80.8 100.4 %all-gather.2.cloned.1.call-start = ((), (), s32[]{:S(2)}) async-start(), calls=%async_computation.4 | async-start | bytes 4276224 | tf_op jit(solution)/shard_map/all_gather | solution.py:28
  183.5 39.1 %slice-start.3 = ((s8[8908800]{0:T(1024)(128)(4,1)}), s8[4194304]{0:T(1024)(128)(4,1)S(1)}, s32[]{:S(2)}) async-start(s8[8908800]{0:T(1024)(128)(4,1)} %bitcast.61), calls=%async_computation.8 | async-start | bytes 8388608
  183.5 39.1 %slice-start.4 = ((s8[8908800]{0:T(1024)(128)(4,1)}), s8[4194304]{0:T(1024)(128)(4,1)S(1)}, s32[]{:S(2)}) async-start(s8[8908800]{0:T(1024)(128)(4,1)} %bitcast.61), calls=%async_computation.9 | async-start | bytes 8388608
  203.0 19.6 %slice-start.5 = ((s8[8908800]{0:T(1024)(128)(4,1)}), s8[520192]{0:T(1024)(128)(4,1)S(1)}, s32[]{:S(2)}) async-start(s8[8908800]{0:T(1024)(128)(4,1)} %bitcast.61), calls=%async_computation.10 | async-start | bytes 1040384
  267.3 8.6 %copy-start.4 = (s32[600]{0:T(1024)S(1)}, s32[600]{0:T(1024)}, u32[]{:S(2)}) copy-start(s32[600]{0:T(1024)} %param.10) | copy-start | bytes 7204
  270.0 23.1 %all-to-all-start.1 = ((f32[16,16,1050]{2,1,0:T(8,128)}), f32[16,16,1050]{2,1,0:T(8,128)}, u32[]{:S(2)}, u32[]{:S(2)}) async-start(f32[16,16,1050]{2,1,0:T(8,128)} %copy.36), calls=%async_computation.1 | async-start | bytes 2359296 | tf_op jit(solution)/shard_map/all_to_all | solution.py:18
  295.3 15.4 %all-to-all-start.2 = ((f32[8,16,1050]{2,1,0:T(8,128)}), f32[8,16,1050]{2,1,0:T(8,128)}, u32[]{:S(2)}, u32[]{:S(2)}) async-start(f32[8,16,1050]{2,1,0:T(8,128)} %broadcast_in_dim.31), calls=%async_computation.2 | async-start | bytes 1179648 | tf_op jit(solution)/shard_map/all_to_all | solution.py:39
Sparse Core Ops, SparseCore 0:
  114.3 66.8 all-gather.1
where the time goes:
time: 367 us; the launch traced here: 362 us
  matrix products  151 us (41%)
  waiting for transfers between devices  116 us (32%)
  local copies, waits for them, and re-layouts  47.9 us (13%)
  starting transfers between devices  18.1 us (5%)
  between operations  13.8 us (4%)
  blocking collectives  10.1 us (3%)
  other arithmetic  5.21 us (1%)
    all_gather x1, waiting for transfers between devices, side_by_side(): lax.all_gather(both, axis, axis=dim, tiled=True)  67 us
    all_to_all x2, waiting for transfers between devices, sum_at_owner(): lax.all_to_all(pieces, axis, split_axis=0, concat_axis=0, tiled=True)  37.8 us
    gather x2, local copies, waits for them, and re-layouts, shards(): permuted = jnp.take(gathered, pick_index, axis=1)  22.2 us
    dot_general x1, matrix products, shards(): jnp.einsum('cpw,wsp->csw', field_imag, spec_imag, precision=highest, pref...  19.5 us
    dot_general x1, matrix products, shards(): jnp.einsum('cpw,wsp->csw', field_real, spec_imag, precision=highest, pref...  19.5 us
    dot_general x1, matrix products, shards(): jnp.einsum('cpw,wsp->csw', field_real, spec_real, precision=highest, pref...  14.8 us
    dot_general x1, matrix products, shards(): jnp.einsum('cpw,wsp->csw', field_imag, spec_real, precision=highest, pref...  14.4 us
    dot_general x1, matrix products, shards(): jnp.einsum('csw,wsp->cpw', rec_imag, spec_imag, precision=highest, prefer...  13.6 us
  transfers between devices with their start and end apart: 4, of which 4 were waited for; matrix products, arithmetic and copies ran while one was open for 2% of the time, Pallas kernels for 0%

commit v1 on v0

v1 whole, which is shorter than its diff:
```python
import functools
import math

import jax
import jax.numpy as jnp
import ml_dtypes
import numpy as np
from jax import lax
from jax.experimental import pallas as pl
from jax.experimental.pallas import tpu as pltpu
from jax.sharding import PartitionSpec as P

MESH = pl.DeviceIdType.MESH
F32, BF16 = jnp.float32, jnp.bfloat16
VMEM = pl.BlockSpec(memory_space=pltpu.VMEM)
ANY = pl.BlockSpec(memory_space=pl.ANY)

COLS, NT, NF = 16, 224, 225
SD, PD = 75, 128
SPAD = 80
FR = 232
ROWS2 = 2 * COLS
CHUNK = 25
NCHUNK = NF // CHUNK
UNROLL = 5


def split_np(table):
    high = table.astype(np.float32).astype(ml_dtypes.bfloat16)
    low = (table - high.astype(np.float64)).astype(np.float32).astype(ml_dtypes.bfloat16)
    return high, low


def tables():
    length = 2 * NT
    w = np.arange(NF)
    t = np.arange(NT)
    phase = (np.outer(w, t) % length) * (2.0 * math.pi / length)
    fwd = np.zeros((2 * FR, NT))
    fwd[:NF] = np.cos(phase)
    fwd[FR : FR + NF] = -np.sin(phase)
    weight = np.where((w == 0) | (w == NT), 1.0, 2.0) / length
    inv = np.zeros((NT, 512))
    inv[:, :NF] = np.cos(phase).T * weight
    inv[:, 256 : 256 + NF] = -np.sin(phase).T * weight
    return (*split_np(fwd), *split_np(inv))


def split(x):
    high = x.astype(BF16)
    return high, (x - high.astype(F32)).astype(BF16)


def dot(a, b, dims=((1,), (0,))):
    return lax.dot_general(a, b, (dims, ((), ())), preferred_element_type=F32)


NT_DIMS = ((1,), (1,))
LIMIT = 60 * 2**20


def dot3(a, b, dims=((1,), (0,))):
    return dot(a[0], b[0], dims) + (dot(a[1], b[0], dims) + dot(a[0], b[1], dims))


def params(**more):
    return pltpu.CompilerParams(vmem_limit_bytes=LIMIT, **more)


def start_specs(sr_hbm, si_hbm, sr, si, sems):
    @pl.loop(0, SD)
    def _(s):
        pltpu.make_async_copy(sr_hbm.at[s], sr.at[:, s, :], sems.at[0]).start()
        pltpu.make_async_copy(si_hbm.at[s], si.at[:, s, :], sems.at[1]).start()


def wait_specs(sr_hbm, si_hbm, sr, si, sems):
    blank = jnp.zeros((CHUNK, SPAD - SD, PD), F32)

    @pl.loop(0, NCHUNK)
    def _(i):
        sr[pl.ds(i * CHUNK, CHUNK), SD:SPAD, :] = blank
        si[pl.ds(i * CHUNK, CHUNK), SD:SPAD, :] = blank

    @pl.loop(0, SD)
    def _(s):
        pltpu.make_async_copy(sr_hbm.at[s], sr.at[:, s, :], sems.at[0]).wait()
        pltpu.make_async_copy(si_hbm.at[s], si.at[:, s, :], sems.at[1]).wait()


def over_frequencies(step):
    @pl.loop(0, NF // UNROLL)
    def _(j):
        for u in range(UNROLL):
            step(j * UNROLL + u)


def part_rows(c):
    return (c, COLS + c)


def to_samples(yn, idh, idl, q):
    total = None
    for part in range(2):
        both = split(jnp.concatenate([yn[part * COLS + 2 * q], yn[part * COLS + 2 * q + 1]], axis=1))
        table = (idh[:, part * 256 : (part + 1) * 256], idl[:, part * 256 : (part + 1) * 256])
        term = dot3(table, both)
        total = term if total is None else total + term
    return total


def put_spectrum(xn, x, res, q, sem):
    for half in range(2):
        for part, row in enumerate(part_rows(2 * q + half)):
            xn[row, 0:FR, :] = res[part * FR : (part + 1) * FR, half * 128 : (half + 1) * 128]
            pltpu.make_async_copy(xn.at[row, pl.ds(0, NF)], x.at[:, row, :], sem).start()


def wait_rows(xn, x, sem):
    @pl.loop(0, ROWS2)
    def _(row):
        pltpu.make_async_copy(xn.at[row, pl.ds(0, NF)], x.at[:, row, :], sem).wait()


def start_columns(y, yn, sems):
    @pl.loop(0, COLS // 2)
    def _(q):
        for half in range(2):
            for row in part_rows(2 * q + half):
                pltpu.make_async_copy(y.at[:, row, :], yn.at[row, pl.ds(0, NF)], sems.at[q]).start()


def wait_columns(y, yn, sems, q):
    for half in range(2):
        for row in part_rows(2 * q + half):
            pltpu.make_async_copy(y.at[:, row, :], yn.at[row, pl.ds(0, NF)], sems.at[q]).wait()


def clear_tails(yn):
    @pl.loop(0, ROWS2)
    def _(row):
        yn[row, NF:256, :] = jnp.zeros((256 - NF, 128), F32)


def adjoint_kernel(
    rec_in, sr_hbm, si_hbm, fdh, fdl, idh, idl, out, sr, si, x, y, xn, flat, rec, sems, rsem, xsem, ysem
):
    start_specs(sr_hbm, si_hbm, sr, si, sems)
    flat[0] = rec_in[:, :, 0:128]
    flat[1, :, :, 0 : NT - 128] = rec_in[:, :, 128:NT]

    def row_copy(side, c):
        return pltpu.make_async_copy(
            flat.at[side, :, c, :], rec.at[side, c, pl.ds(0, SD)], rsem.at[side]
        )

    @pl.loop(0, COLS)
    def _(c):
        row_copy(0, c).start()
        row_copy(1, c).start()
        rec[0, c, SD:128, :] = jnp.zeros((128 - SD, 128), F32)
        rec[1, c, SD:128, :] = jnp.zeros((128 - SD, 128), F32)

    @pl.loop(0, COLS)
    def _(c):
        row_copy(0, c).wait()
        row_copy(1, c).wait()

    @pl.loop(0, COLS // 2)
    def _(q):
        sides = [rec[side, pl.ds(2 * q, 2)].reshape(256, 128) for side in range(2)]
        both = split(jnp.concatenate([sides[0], sides[1][:, : NT - 128]], axis=1))
        put_spectrum(xn, x, dot3((fdh[...], fdl[...]), both, NT_DIMS), q, xsem)

    wait_rows(xn, x, xsem)
    wait_specs(sr_hbm, si_hbm, sr, si, sems)
    clear_tails(xn)

    def step(w):
        ah, al = split(x[w][:, :SPAD])
        both = split(jnp.concatenate([sr[w], si[w]], axis=1))
        wide = dot(jnp.concatenate([ah, al], axis=0), both[0])
        p = wide[:ROWS2] + (wide[ROWS2:] + dot(ah, both[1]))
        y[w] = jnp.concatenate(
            [p[:COLS, :PD] + p[COLS:, PD:], p[COLS:, :PD] - p[:COLS, PD:]], axis=0
        )

    over_frequencies(step)
    start_columns(y, xn, ysem)

    @pl.loop(0, COLS // 2)
    def _(q):
        wait_columns(y, xn, ysem, q)
        res = to_samples(xn, idh, idl, q)
        out[2 * q] = res[:, :PD]
        out[2 * q + 1] = res[:, PD:]


def forward_kernel(
    adj, prior, sr_hbm, si_hbm, fdh, fdl, idh, idl, out, sr, si, x, y, xn, on, ph, pl_, sems, xsem, ysem, osem
):
    start_specs(sr_hbm, si_hbm, sr, si, sems)
    high, low = split(dot3((fdh[...], fdl[...]), split(prior[...])))
    ph[...] = high
    pl_[...] = low

    @pl.loop(0, COLS // 2)
    def _(q):
        both = split(jnp.concatenate([adj[2 * q], adj[2 * q + 1]], axis=1))
        put_spectrum(xn, x, dot3((ph[...], pl_[...]), both), q, xsem)

    wait_rows(xn, x, xsem)
    wait_specs(sr_hbm, si_hbm, sr, si, sems)
    clear_tails(xn)

    def step(w):
        fh, fl = split(x[w])
        left = jnp.concatenate(
            [jnp.concatenate([fh, fh], axis=1), jnp.concatenate([fl, jnp.zeros_like(fl)], axis=1)],
            axis=0,
        )
        prods = []
        for s in (sr, si):
            wide = dot(left, jnp.concatenate(split(s[w]), axis=1), NT_DIMS)
            prods.append(wide[:ROWS2] + wide[ROWS2:])
        p, r = prods
        both = jnp.concatenate([p[:COLS] - r[COLS:], p[COLS:] + r[:COLS]], axis=0)
        y[w] = jnp.concatenate([both, jnp.zeros((ROWS2, 128 - SPAD), F32)], axis=1)

    over_frequencies(step)
    start_columns(y, xn, ysem)

    @pl.loop(0, COLS // 2)
    def _(q):
        wait_columns(y, xn, ysem, q)
        res = to_samples(xn, idh, idl, q)
        for half in range(2):
            on[2 * q + half] = res[:, half * 128 : (half + 1) * 128]
            pltpu.make_async_copy(on.at[2 * q + half], out.at[:, 2 * q + half, :], osem).start()

    @pl.loop(0, COLS)
    def _(c):
        pltpu.make_async_copy(on.at[c], out.at[:, c, :], osem).wait()


def spec_scratch():
    return [
        pltpu.VMEM((NF, SPAD, PD), F32),
        pltpu.VMEM((NF, SPAD, PD), F32),
        pltpu.VMEM((NF, ROWS2, 128), F32),
        pltpu.VMEM((NF, ROWS2, 128), F32),
        pltpu.VMEM((ROWS2, 256, 128), F32),
    ]


def adjoint_call(rec, sr, si, tabs):
    return pl.pallas_call(
        adjoint_kernel,
        out_shape=jax.ShapeDtypeStruct((COLS, NT, PD), F32),
        in_specs=[VMEM, ANY, ANY] + [VMEM] * 4,
        out_specs=VMEM,
        scratch_shapes=spec_scratch()
        + [
            pltpu.VMEM((2, SD, COLS, 128), F32),
            pltpu.VMEM((2, COLS, 128, 128), F32),
            pltpu.SemaphoreType.DMA((2,)),
            pltpu.SemaphoreType.DMA((2,)),
            pltpu.SemaphoreType.DMA,
            pltpu.SemaphoreType.DMA((COLS // 2,)),
        ],
        compiler_params=params(),
        name="adjoint",
    )(rec, sr, si, *tabs)


def forward_call(adj, prior, sr, si, tabs):
    return pl.pallas_call(
        forward_kernel,
        out_shape=jax.ShapeDtypeStruct((NT, COLS, 128), F32),
        in_specs=[VMEM, VMEM, ANY, ANY] + [VMEM] * 4,
        out_specs=VMEM,
        scratch_shapes=spec_scratch()
        + [pltpu.VMEM((COLS, NT, 128), F32)]
        + [pltpu.VMEM((2 * FR, NT), BF16)] * 2
        + [
            pltpu.SemaphoreType.DMA((2,)),
            pltpu.SemaphoreType.DMA,
            pltpu.SemaphoreType.DMA((COLS // 2,)),
            pltpu.SemaphoreType.DMA,
        ],
        compiler_params=params(),
        name="forward",
    )(adj, prior, sr, si, *tabs)


def update_kernel(place, gath, inv_hbm, out, inv, perm, sem):
    copy = pltpu.make_async_copy(inv_hbm, inv, sem)
    copy.start()
    steps, rows, keys = inv.shape
    where = place[...]

    @pl.loop(0, gath.shape[0] // 2)
    def _(i):
        row = lax.broadcasted_iota(jnp.int32, (256, keys), 0) + i * 256
        pick = (row == where).astype(F32).astype(BF16)
        high, low = split(jnp.concatenate([gath[2 * i], gath[2 * i + 1]], axis=1))
        term = dot(high, pick) + dot(low, pick)

        @pl.when(i == 0)
        def _():
            perm[...] = term

        @pl.when(i > 0)
        def _():
            perm[...] += term

    copy.wait()
    out[...] = jnp.zeros_like(out)

    @pl.loop(0, steps)
    def _(t):
        at = pl.ds(pl.multiple_of(t * COLS, COLS), COLS)
        out[:, 0:rows] += dot3(split(perm[at, :]), split(inv[t]), NT_DIMS)


def update_call(place, gath, inv):
    return pl.pallas_call(
        update_kernel,
        out_shape=jax.ShapeDtypeStruct((COLS, 128), F32),
        in_specs=[VMEM, VMEM, ANY],
        out_specs=VMEM,
        scratch_shapes=[
            pltpu.VMEM(inv.shape, F32),
            pltpu.VMEM((gath.shape[1], inv.shape[2]), F32),
            pltpu.SemaphoreType.DMA,
        ],
        compiler_params=params(),
        name="update",
    )(place, gath, inv)


def here():
    sens, par = lax.axis_index("sens"), lax.axis_index("par")
    return sens // 2, sens % 2, par // 8, par // 2 % 4, par % 2


def device(x, y_hi, y_lo, z, core):
    return (x * 2 + y_hi, y_lo * 8 + z * 2 + core)


def greet(devices):
    barrier = pltpu.get_barrier_semaphore()
    for d in devices:
        pl.semaphore_signal(barrier, inc=1, device_id=d, device_id_type=MESH)
    pl.semaphore_wait(barrier, len(devices))


class Sender:
    def __init__(self, send_sems, recv_sems):
        self.send_sems, self.recv_sems, self.sent = send_sems, recv_sems, []

    def __call__(self, src, dst, to):
        k = len(self.sent)
        copy = pltpu.make_async_remote_copy(
            src_ref=src,
            dst_ref=dst,
            send_sem=self.send_sems.at[k],
            recv_sem=self.recv_sems.at[k],
            device_id=to,
            device_id_type=MESH,
        )
        copy.start()
        self.sent.append(copy)
        return copy

    def finish(self):
        for copy in self.sent:
            copy.wait_send()


def rows_at(start, size):
    return pl.ds(pl.multiple_of(start, 8), size)


class RingSum:
    def __init__(self, send, data, at, place, up, down, relay, arrive):
        self.send, self.data, self.at, self.place = send, data, at, place
        self.up, self.down, self.relay, self.arrive = up, down, relay, arrive
        nxt, prv, far = (place + 1) % 4, (place + 3) % 4, (place + 2) % 4
        self.nxt, self.prv = nxt, prv
        self.far_up = send(data.at[at(far, 0)], relay.at[0], up)
        self.far_down = send(data.at[at(far, 1)], relay.at[1], down)
        self.near_up = send(data.at[at(nxt, 1)], arrive.at[0], up)
        self.near_down = send(data.at[at(prv, 0)], arrive.at[1], down)

    def pass_on(self):
        self.far_up.wait_recv()
        self.relay[0] = self.relay[0] + self.data[self.at(self.nxt, 0)]
        self.last_up = self.send(self.relay.at[0], self.arrive.at[2], self.up)
        self.far_down.wait_recv()
        self.relay[1] = self.relay[1] + self.data[self.at(self.prv, 1)]
        self.last_down = self.send(self.relay.at[1], self.arrive.at[3], self.down)

    def half(self, h):
        (self.near_down, self.near_up)[h].wait_recv()
        (self.last_up, self.last_down)[h].wait_recv()
        own = self.data[self.at(self.place, h)]
        return own + self.arrive[(1, 0)[h]] + self.arrive[(2, 3)[h]]


class RingSpread:
    def __init__(self, send, data, at, place, up, down):
        self.send, self.data, self.at, self.place, self.up, self.down = send, data, at, place, up, down
        mine = [data.at[at(place, h)] for h in range(2)]
        self.first_up = send(mine[0], mine[0], up)
        self.first_down = send(mine[1], mine[1], down)
        self.second_up = send(mine[1], mine[1], up)
        self.second_down = send(mine[0], mine[0], down)

    def pass_on(self):
        self.first_up.wait_recv()
        piece = self.data.at[self.at((self.place + 3) % 4, 0)]
        self.far_up = self.send(piece, piece, self.up)
        self.first_down.wait_recv()
        piece = self.data.at[self.at((self.place + 1) % 4, 1)]
        self.far_down = self.send(piece, piece, self.down)

    def finish(self):
        for copy in (self.second_up, self.second_down, self.far_up, self.far_down):
            copy.wait_recv()


def sum_all_kernel(a, out, relay_a, arrive_a, swap_a, relay_b, arrive_b, swap_b, half_b, done_a, ssem, rsem):
    x, y_hi, y_lo, z, core = here()
    up = device((x + 1) % 4, y_hi, y_lo, z, core)
    down = device((x + 3) % 4, y_hi, y_lo, z, core)
    over = device(x, 1 - y_hi, y_lo, z, core)
    greet([up, down, over])
    send = Sender(ssem, rsem)
    half_a = relay_a.shape[1]
    quarter_b = relay_b.shape[1]
    start_b = 8 * half_a
    size_b = 8 * quarter_b

    def at_a(q, h):
        return rows_at((2 * q + h) * half_a, half_a)

    def at_half_b(q, h):
        return rows_at((2 * q + h) * quarter_b, quarter_b)

    def at_b(y):
        def at(q, h):
            return rows_at(start_b + y * size_b + (2 * q + h) * quarter_b, quarter_b)

        return at

    theirs = rows_at(start_b + (1 - y_hi) * size_b, size_b)
    ours = rows_at(start_b + y_hi * size_b, size_b)
    to_over_b = send(a.at[theirs], swap_b, over)
    ring_a = RingSum(send, a, at_a, x, up, down, relay_a, arrive_a)
    ring_a.pass_on()
    to_over_b.wait_recv()
    half_b[...] = a[ours] + swap_b[...]
    ring_b = RingSum(send, half_b, at_half_b, x, up, down, relay_b, arrive_b)
    for h in range(2):
        done_a[h] = ring_a.half(h)
    to_over_a = send(done_a.at[1 - y_hi], swap_a, over)
    ring_b.pass_on()
    to_over_a.wait_recv()
    mine = at_a(x, y_hi)
    out[mine] = done_a[y_hi] + swap_a[...]
    back_a = send(out.at[mine], out.at[mine], over)
    place_b = at_b(y_hi)
    for h in range(2):
        out[place_b(x, h)] = ring_b.half(h)
    spread_b = RingSpread(send, out, place_b, x, up, down)
    back_a.wait_recv()
    spread_a = RingSpread(send, out, at_a, x, up, down)
    spread_b.pass_on()
    spread_b.finish()
    back_b = send(out.at[ours], out.at[ours], over)
    spread_a.pass_on()
    spread_a.finish()
    back_b.wait_recv()
    send.finish()


def sum_all_call(a):
    rows = a.shape[0]
    half_a = 272
    quarter_b = (rows - 8 * half_a) // 16
    return pl.pallas_call(
        sum_all_kernel,
        out_shape=jax.ShapeDtypeStruct(a.shape, F32),
        in_specs=[VMEM],
        out_specs=VMEM,
        scratch_shapes=[
            pltpu.VMEM((2, half_a, 128), F32),
            pltpu.VMEM((4, half_a, 128), F32),
            pltpu.VMEM((half_a, 128), F32),
            pltpu.VMEM((2, quarter_b, 128), F32),
            pltpu.VMEM((4, quarter_b, 128), F32),
            pltpu.VMEM((8 * quarter_b, 128), F32),
            pltpu.VMEM((8 * quarter_b, 128), F32),
            pltpu.VMEM((2, half_a, 128), F32),
            pltpu.SemaphoreType.DMA((32,)),
            pltpu.SemaphoreType.DMA((32,)),
        ],
        compiler_params=params(collective_id=0, has_side_effects=True),
        name="sum_all",
    )(a)


def sum_times_kernel(p, out, core_in, mine, relay, arrive, own, swap, ssem, rsem):
    x, y_hi, y_lo, z, core = here()
    up = device((x + 1) % 4, y_hi, y_lo, z, core)
    down = device((x + 3) % 4, y_hi, y_lo, z, core)
    over = device(x, 1 - y_hi, y_lo, z, core)
    next_z = device(x, y_hi, y_lo, (z + 1) % 4, core)
    last_z = device(x, y_hi, y_lo, (z + 3) % 4, core)
    beside = device(x, y_hi, 1 - y_lo, z, core)
    partner = device(x, y_hi, y_lo, z, 1 - core)
    greet([up, down, over, next_z, last_z, beside, partner])
    send = Sender(ssem, rsem)
    order = [(h, (z + d) % 4) for d, h in ((2, 0), (2, 1), (1, 1), (3, 0), (1, 0), (3, 1), (0, 0), (0, 1))]
    swaps = [send(p.at[4 * h + q, 1 - core], core_in.at[4 * h + q], partner) for h, q in order]
    for copy, (h, q) in zip(swaps, order):
        m = 4 * h + q
        copy.wait_recv()
        mine[m] = p[m, core] + core_in[m]
    ring = RingSum(send, mine, lambda q, h: 4 * h + q, z, next_z, last_z, relay, arrive)
    ring.pass_on()
    for h in range(2):
        own[h] = ring.half(h)
    to_beside = send(own.at[1 - y_lo], swap, beside)
    to_beside.wait_recv()
    sens = 2 * x + y_hi
    out[sens] = own[y_lo] + swap[...]
    rows = out.shape[1]

    def at(y):
        return lambda q, h: (2 * q + y, pl.ds(h * (rows // 2), rows // 2))

    back = send(out.at[sens], out.at[sens], over)
    near = RingSpread(send, out, at(y_hi), x, up, down)
    near.pass_on()
    back.wait_recv()
    far = RingSpread(send, out, at(1 - y_hi), x, up, down)
    near.finish()
    far.pass_on()
    far.finish()
    send.finish()


def sum_times_call(p):
    rows = p.shape[2]
    block = (rows, 128)
    return pl.pallas_call(
        sum_times_kernel,
        out_shape=jax.ShapeDtypeStruct((8, *block), F32),
        in_specs=[VMEM],
        out_specs=VMEM,
        scratch_shapes=[
            pltpu.VMEM((8, *block), F32),
            pltpu.VMEM((8, *block), F32),
            pltpu.VMEM((2, *block), F32),
            pltpu.VMEM((4, *block), F32),
            pltpu.VMEM((2, *block), F32),
            pltpu.VMEM(block, F32),
            pltpu.SemaphoreType.DMA((32,)),
            pltpu.SemaphoreType.DMA((32,)),
        ],
        compiler_params=params(collective_id=1, has_side_effects=True),
        name="sum_times",
    )(p)


def finish_kernel(u, out, rows, recv, ssem, rsem):
    n = u.shape[0]
    sens, me = lax.axis_index("sens"), lax.axis_index("par")
    others = [(me + d) % n for d in range(1, n)]
    greet([(sens, j) for j in others])
    for c in range(n):
        rows[c] = jnp.broadcast_to(u[c : c + 1, :], (8, 128))
    send = Sender(ssem, rsem)
    for d, j in enumerate(others):
        send(rows.at[j], recv.at[d], (sens, j))
    total = rows[me]
    for d, copy in enumerate(send.sent):
        copy.wait_recv()
        total = total + recv[d]
    out[...] = total[0:1, 0 : out.shape[1]]
    send.finish()


def finish_call(u, width):
    n = u.shape[0]
    return pl.pallas_call(
        finish_kernel,
        out_shape=jax.ShapeDtypeStruct((1, width), F32),
        in_specs=[VMEM],
        out_specs=VMEM,
        scratch_shapes=[
            pltpu.VMEM((n, 8, 128), F32),
            pltpu.VMEM((n - 1, 8, 128), F32),
            pltpu.SemaphoreType.DMA((n - 1,)),
            pltpu.SemaphoreType.DMA((n - 1,)),
        ],
        compiler_params=params(collective_id=2, has_side_effects=True),
        name="finish",
    )(u)


def shards(records, spec_real, spec_imag, prior_cov, sensor_map, inverse_rows):
    tabs = tables()
    sr, si = spec_real.transpose(1, 0, 2), spec_imag.transpose(1, 0, 2)
    place = (sensor_map // SD * 128 + sensor_map % SD).astype(jnp.int32)[None]
    a = adjoint_call(records.transpose(1, 0, 2), sr, si, tabs)
    a = sum_all_call(a.reshape(COLS * NT, PD)).reshape(COLS, NT, PD)
    p = forward_call(a, prior_cov, sr, si, tabs)
    g = sum_times_call(p.reshape(8, 2, NT, 128))
    u = update_call(place, g, inverse_rows.transpose(1, 0, 2))
    return finish_call(u, inverse_rows.shape[0])


def solution(mesh):
    return jax.shard_map(
        shards,
        mesh=mesh,
        in_specs=(
            P(None, "sens", None),
            P(None, "sens", "par"),
            P(None, "sens", "par"),
            P(),
            P(),
            P("sens", "par", None),
        ),
        out_specs=P("par", "sens"),
        check_vma=False,
    )
```

time: 367 us -> 160 us (0.44); the launches traced: 362 us -> 159 us
  Pallas kernels: 0 us -> 158 us
  matrix products: 151 us -> 0 us
  waiting for transfers between devices: 116 us -> 0 us
  local copies, waits for them, and re-layouts: 47.9 us -> 1.69 us
  starting transfers between devices: 18.1 us -> 0 us
  between operations: 13.8 us -> 0.07 us
  blocking collectives: 10.1 us -> 0 us
  other arithmetic: 5.21 us -> 0.02 us
    pallas_call x0 -> x6, Pallas kernels: none -> 158 us  [the longest x1 39.5 us: sum_all_call(): pl.pallas_call(sum_all_kernel, out_shape=jax.ShapeDtypeStruct(a.shape, F3...]
    dot_general x19 -> x0, matrix products: 151 us -> none  [the longest x1 19.5 us: shards(): jnp.einsum('cpw,wsp->csw', field_imag, spec_imag, precision=highest, pref...]
    all_gather x1 -> x0, waiting for transfers between devices: 67 us -> none  [side_by_side(): lax.all_gather(both, axis, axis=dim, tiled=True)]
    all_to_all x3 -> x0, waiting for transfers between devices: 48.6 us -> none  [the longest x2 37.8 us: sum_at_owner(): lax.all_to_all(pieces, axis, split_axis=0, concat_axis=0, tiled=True)]
    gather x2 -> x0, local copies, waits for them, and re-layouts: 22.2 us -> none  [shards(): permuted = jnp.take(gathered, pick_index, axis=1)]
    all_to_all x3 -> x0, starting transfers between devices: 17.7 us -> none  [the longest x2 13.3 us: sum_at_owner(): lax.all_to_all(pieces, axis, split_axis=0, concat_axis=0, tiled=True)]
    all_to_all x1 -> x0, blocking collectives: 10.1 us -> none  [sum_at_owner(): lax.all_to_all(pieces, axis, split_axis=0, concat_axis=0, tiled=True)]
    dot_general x2 -> x0, local copies, waits for them, and re-layouts: 5.9 us -> none  [the longest x1 3.09 us: to_spectrum(): jnp.dot(signal, cosine, precision=highest, preferred_element_type=jnp.flo...]
  transfers between devices with their start and end apart: 4 -> 0, of which waited for: 4 -> 0; matrix products, arithmetic and copies ran while one was open for 2% -> 0% of each run, Pallas kernels for 0% -> 0%
where the time goes in v1:
time: 160 us; the launch traced here: 159 us
  Pallas kernels  158 us (99%)
  local copies, waits for them, and re-layouts  1.69 us (1%)
    pallas_call x1, Pallas kernels, sum_all_call(): pl.pallas_call(sum_all_kernel, out_shape=jax.ShapeDtypeStruct(a.shape, F3...  39.5 us
    pallas_call x1, Pallas kernels, sum_times_call(): pl.pallas_call(sum_times_kernel, out_shape=jax.ShapeDtypeStruct((8, *bloc...  38.1 us
    pallas_call x1, Pallas kernels, forward_call(): pl.pallas_call(forward_kernel, out_shape=jax.ShapeDtypeStruct((NT, COLS,...  32.3 us
    pallas_call x1, Pallas kernels, adjoint_call(): pl.pallas_call(adjoint_kernel, out_shape=jax.ShapeDtypeStruct((COLS, NT,...  30.3 us
    pallas_call x1, Pallas kernels, finish_call(): pl.pallas_call(finish_kernel, out_shape=jax.ShapeDtypeStruct((1, width),...  10.1 us
    pallas_call x1, Pallas kernels, update_call(): pl.pallas_call(update_kernel, out_shape=jax.ShapeDtypeStruct((COLS, 128),...  7.25 us

profile of v1, /device:TPU:1, one launch (start us, length us, event | category | flops | bytes accessed | tf_op | source)
XLA Modules:
  0.0 159.3 jit_solution(1813626708434566428)
XLA Ops:
  0.0 30.3 %adjoint.1 = f32[16,224,128]{2,1,0:T(8,128)} custom-call(f32[75,16,224]{2,1,0:T(8,128)} %bitcast.15, f32[75,225,128]{2,1,0:T(8,128)} %bitcast.7, f32[75,225,128]{2,1,0:T(8,128)} %bitcast.9, bf16[464,224]{1,0:T(8,128)(2,1)} %constant.30.clone.fdh, bf16[464,224]{1,0:T(8,128)(2,1)} %constant.31.clone.fdl, bf16[224,512]{1,0:T(8,128)(2,1)} %constant.32.clone.idh, ...), custom_call_target="tpu_custom_call" | custom-call | tf_op jit(solution)/shard_map/adjoint/pallas_call | solution.py:257
  30.3 39.5 %sum_all.1 = f32[3584,128]{1,0:T(8,128)} custom-call(f32[3584,128]{1,0:T(8,128)} %bitcast.12), custom_call_target="tpu_custom_call" | custom-call | tf_op jit(solution)/shard_map/sum_all/pallas_call | solution.py:492
  69.8 32.3 %forward.1 = f32[224,16,128]{2,1,0:T(8,128)} custom-call(f32[16,224,128]{2,1,0:T(8,128)} %bitcast.11, f32[224,224]{1,0:T(8,128)} %prior.1, f32[75,225,128]{2,1,0:T(8,128)} %bitcast.8, f32[75,225,128]{2,1,0:T(8,128)} %bitcast.10, bf16[464,224]{1,0:T(8,128)(2,1)} %constant.30.clone.fdh, bf16[464,224]{1,0:T(8,128)(2,1)} %constant.31.clone.fdl, ...), custom_call_target="tpu_custom_call" | custom-call | tf_op jit(solution)/shard_map/forward/pallas_call | solution.py:277
  102.1 0.0 copy-start
  102.1 38.1 %sum_times.1.gath = f32[8,224,128]{2,1,0:T(8,128)} custom-call(f32[8,2,224,128]{3,2,1,0:T(8,128)} %bitcast.13), custom_call_target="tpu_custom_call" | custom-call | tf_op jit(solution)/shard_map/sum_times/pallas_call | solution.py:558
  140.2 0.0 copy-done
  140.2 0.6 broadcast_in_dim.3.place
  140.8 7.2 %update.1.u = f32[16,128]{1,0:T(8,128)} custom-call(s32[1,600]{1,0:T(1,128)} %broadcast_in_dim.3.place, f32[8,224,128]{2,1,0:T(8,128)} %sum_times.1.gath, f32[14,96,600]{2,1,0:T(8,128)} %bitcast.14), custom_call_target="tpu_custom_call" | custom-call | tf_op jit(solution)/shard_map/update/pallas_call | solution.py:327
  148.1 10.1 %finish.1 = f32[1,96]{1,0:T(1,128)} custom-call(f32[16,128]{1,0:T(8,128)} %update.1.u), custom_call_target="tpu_custom_call" | custom-call | tf_op jit(solution)/shard_map/finish/pallas_call | solution.py:598
  158.2 1.1 copy.12
  (1 shorter events, 0.0 us)
Async XLA Ops:
  102.1 38.1 %copy-start = (s32[600]{0:T(1024)S(1)}, s32[600]{0:T(1024)}, u32[]{:S(2)}) copy-start(s32[600]{0:T(1024)} %param.14) | copy-start | bytes 7204

commit v2 on v0

v2 whole, which is shorter than its diff:
```python
import functools
import math

import jax
import jax.numpy as jnp
import ml_dtypes
import numpy as np
from jax import lax
from jax.experimental import pallas as pl
from jax.experimental.pallas import tpu as pltpu
from jax.sharding import PartitionSpec as P

MESH = pl.DeviceIdType.MESH
F32, BF16 = jnp.float32, jnp.bfloat16
VMEM = pl.BlockSpec(memory_space=pltpu.VMEM)
ANY = pl.BlockSpec(memory_space=pl.ANY)
HBM = pl.BlockSpec(memory_space=pltpu.HBM)

COLS, NT, NF = 16, 224, 225
SD, PD = 75, 128
SPAD = 80
FR = 232
ROWS2 = 2 * COLS
CHUNK = 25
NCHUNK = NF // CHUNK
UNROLL = 25
BLOCKS, STEPS, SPADT = 16, 14, 16
GROUP = 8
WIDE = GROUP * SPAD
HALVES = 2
HALF_ROWS = COLS * NT // HALVES
HALF_A, QUARTER_B = 128, 48
NT_DIMS = ((1,), (1,))
LIMIT = 60 * 2**20


def split_np(table):
    high = table.astype(np.float32).astype(ml_dtypes.bfloat16)
    low = (table - high.astype(np.float64)).astype(np.float32).astype(ml_dtypes.bfloat16)
    return high, low


def thrice_np(table):
    pieces = []
    for at in range(0, table.shape[1], 256):
        high, low = split_np(table[:, at : at + 256])
        pieces += [high, low, high]
    return np.concatenate(pieces, axis=1)


def tables():
    length = 2 * NT
    w = np.arange(NF)
    t = np.arange(NT)
    phase = (np.outer(w, t) % length) * (2.0 * math.pi / length)
    fwd = np.zeros((2 * FR, 256))
    fwd[:NF, :NT] = np.cos(phase)
    fwd[FR : FR + NF, :NT] = -np.sin(phase)
    weight = np.where((w == 0) | (w == NT), 1.0, 2.0) / length
    inv = np.zeros((NT, 512))
    inv[:, :NF] = np.cos(phase).T * weight
    inv[:, 256 : 256 + NF] = -np.sin(phase).T * weight
    blocks = np.zeros((BLOCKS, SPADT, 512))
    blocks[:, :STEPS] = inv.reshape(BLOCKS, STEPS, 512)
    return tuple(thrice_np(table) for table in (fwd, inv, blocks.reshape(-1, 512)))


def split(x):
    high = x.astype(BF16)
    return high, (x - high.astype(F32)).astype(BF16)


def dot(a, b, dims=((1,), (0,))):
    return lax.dot_general(a, b, (dims, ((), ())), preferred_element_type=F32)


def thrice(x, axis):
    high, low = split(x)
    return [jnp.concatenate([high, high, low], axis=axis)]


def dot3(a, b, dims=((1,), (0,))):
    return dot(a[0], b[0], dims) + (dot(a[1], b[0], dims) + dot(a[0], b[1], dims))


def here():
    sens, par = lax.axis_index("sens"), lax.axis_index("par")
    return sens // 2, sens % 2, par // 8, par // 2 % 4, par % 2


def device(x, y_hi, y_lo, z, core):
    return (x * 2 + y_hi, y_lo * 8 + z * 2 + core)


def greet(devices):
    barrier = pltpu.get_barrier_semaphore()
    for d in devices:
        pl.semaphore_signal(barrier, inc=1, device_id=d, device_id_type=MESH)


def all_here(devices):
    pl.semaphore_wait(pltpu.get_barrier_semaphore(), len(devices))


class Sender:
    def __init__(self, send_sems, recv_sems):
        self.send_sems, self.recv_sems, self.sent = send_sems, recv_sems, []

    def __call__(self, src, dst, to):
        k = len(self.sent)
        copy = pltpu.make_async_remote_copy(
            src_ref=src,
            dst_ref=dst,
            send_sem=self.send_sems.at[k],
            recv_sem=self.recv_sems.at[k],
            device_id=to,
            device_id_type=MESH,
        )
        copy.start()
        self.sent.append(copy)
        return copy

    def finish(self):
        for copy in self.sent:
            copy.wait_send()


def rows_at(start, size):
    return pl.ds(pl.multiple_of(start, 8), size)


class RingSum:
    def __init__(self, send, data, at, place, up, down, relay, arrive):
        self.send, self.data, self.at, self.place = send, data, at, place
        self.up, self.down, self.relay, self.arrive = up, down, relay, arrive
        nxt, prv, far = (place + 1) % 4, (place + 3) % 4, (place + 2) % 4
        self.nxt, self.prv = nxt, prv
        self.far_up = send(data.at[at(far, 0)], relay.at[0], up)
        self.far_down = send(data.at[at(far, 1)], relay.at[1], down)
        self.near_up = send(data.at[at(nxt, 1)], arrive.at[0], up)
        self.near_down = send(data.at[at(prv, 0)], arrive.at[1], down)

    def pass_on(self):
        self.far_up.wait_recv()
        self.relay[0] = self.relay[0] + self.data[self.at(self.nxt, 0)]
        self.last_up = self.send(self.relay.at[0], self.arrive.at[2], self.up)
        self.far_down.wait_recv()
        self.relay[1] = self.relay[1] + self.data[self.at(self.prv, 1)]
        self.last_down = self.send(self.relay.at[1], self.arrive.at[3], self.down)

    def half(self, h):
        (self.near_down, self.near_up)[h].wait_recv()
        (self.last_up, self.last_down)[h].wait_recv()
        own = self.data[self.at(self.place, h)]
        return own + self.arrive[(1, 0)[h]] + self.arrive[(2, 3)[h]]


class RingSpread:
    def __init__(self, send, data, at, place, up, down):
        self.send, self.data, self.at, self.place, self.up, self.down = send, data, at, place, up, down
        mine = [data.at[at(place, h)] for h in range(2)]
        self.first_up = send(mine[0], mine[0], up)
        self.first_down = send(mine[1], mine[1], down)
        self.second_up = send(mine[1], mine[1], up)
        self.second_down = send(mine[0], mine[0], down)

    def pass_on(self):
        self.first_up.wait_recv()
        piece = self.data.at[self.at((self.place + 3) % 4, 0)]
        self.far_up = self.send(piece, piece, self.up)
        self.first_down.wait_recv()
        piece = self.data.at[self.at((self.place + 1) % 4, 1)]
        self.far_down = self.send(piece, piece, self.down)

    def finish(self):
        for copy in (self.second_up, self.second_down, self.far_up, self.far_down):
            copy.wait_recv()


PEERS = ((1, 2), (0, 2), (1, 1), (1, 3), (1, 0), (0, 1), (0, 3))


class Refs:
    def __init__(self, names, refs):
        for name, ref in zip(names, refs, strict=True):
            setattr(self, name, ref)


def start_specs(r):
    @pl.loop(0, SD)
    def _(s):
        pltpu.make_async_copy(r.sr_hbm.at[s], r.sr.at[:, s, :], r.spec_sem.at[0]).start()
        pltpu.make_async_copy(r.si_hbm.at[s], r.si.at[:, s, :], r.spec_sem.at[1]).start()

    blank = jnp.zeros((CHUNK, SPAD - SD, PD), F32)

    @pl.loop(0, NCHUNK)
    def _(i):
        r.sr[pl.ds(i * CHUNK, CHUNK), SD:SPAD, :] = blank
        r.si[pl.ds(i * CHUNK, CHUNK), SD:SPAD, :] = blank


def wait_specs(r):
    @pl.loop(0, SD)
    def _(s):
        pltpu.make_async_copy(r.sr_hbm.at[s], r.sr.at[:, s, :], r.spec_sem.at[0]).wait()
        pltpu.make_async_copy(r.si_hbm.at[s], r.si.at[:, s, :], r.spec_sem.at[1]).wait()


def part_rows(c):
    return (c, COLS + c)


def pair_rows(q):
    return [row for half in range(2) for row in part_rows(2 * q + half)]


def out_row(r, row, q):
    return pltpu.make_async_copy(r.xn.at[row, pl.ds(0, NF)], r.rows_hbm.at[row], r.xsem.at[0, q])


def in_row(r, row, q):
    return pltpu.make_async_copy(r.rows_hbm.at[row], r.x.at[:, row, :], r.xsem.at[1, q])


def put_spectrum(r, res, q):
    for half in range(2):
        for part, row in enumerate(part_rows(2 * q + half)):
            r.xn[row, 0:FR, :] = res[part * FR : (part + 1) * FR, half * 128 : (half + 1) * 128]
            out_row(r, row, q).start()


def turn_rows(r, q):
    for row in pair_rows(q):
        out_row(r, row, q).wait()
    for row in pair_rows(q):
        in_row(r, row, q).start()


def spectra(r, first, last, pair_of, table, dims):
    @pl.loop(first, last)
    def _(q):
        both = thrice(pair_of(q), dims[1][0])[0]
        put_spectrum(r, dot(table[...], both, dims), q)

        @pl.when(q > first)
        def _():
            turn_rows(r, q - 1)


def wait_spectra(r):
    @pl.loop(0, COLS // 2)
    def _(q):
        for row in pair_rows(q):
            in_row(r, row, q).wait()

    @pl.loop(0, ROWS2)
    def _(row):
        r.xn[row, NF:256, :] = jnp.zeros((256 - NF, 128), F32)


def out_chunk(r, i):
    at = pl.ds(i * CHUNK, CHUNK)
    return pltpu.make_async_copy(r.y.at[at], r.freq_hbm.at[at], r.ysem.at[i])


def in_column(r, row, q):
    return pltpu.make_async_copy(r.freq_hbm.at[:, row, :], r.xn.at[row, pl.ds(0, NF)], r.csem.at[q])


def over_frequencies(r, step):
    @pl.loop(0, NCHUNK)
    def _(i):
        @pl.loop(0, CHUNK // UNROLL)
        def _(j):
            for u in range(UNROLL):
                step(i * CHUNK + j * UNROLL + u)

        out_chunk(r, i).start()

    @pl.loop(0, NCHUNK)
    def _(i):
        out_chunk(r, i).wait()

    @pl.loop(0, COLS // 2)
    def _(q):
        for row in pair_rows(q):
            in_column(r, row, q).start()


def wait_columns(r, q):
    for row in pair_rows(q):
        in_column(r, row, q).wait()


def to_samples(columns, table):
    both = jnp.concatenate(thrice(columns(0), 0) + thrice(columns(1), 0), axis=0)
    return dot(table[...], both)


def record_pairs(r):
    flat, rec = r.flat, r.rec
    flat[0] = r.rec_in[:, :, 0:128]
    flat[1, :, :, 0 : NT - 128] = r.rec_in[:, :, 128:NT]
    flat[1, :, :, NT - 128 : 128] = jnp.zeros((SD, COLS, 256 - NT), F32)

    def row_copy(side, c):
        return pltpu.make_async_copy(
            flat.at[side, :, c, :], rec.at[side, c, pl.ds(0, SD)], r.rsem.at[side]
        )

    @pl.loop(0, COLS)
    def _(c):
        row_copy(0, c).start()
        row_copy(1, c).start()
        rec[0, c, SD:128, :] = jnp.zeros((128 - SD, 128), F32)
        rec[1, c, SD:128, :] = jnp.zeros((128 - SD, 128), F32)

    @pl.loop(0, COLS)
    def _(c):
        row_copy(0, c).wait()
        row_copy(1, c).wait()

    def pair_of(q):
        sides = [rec[side, pl.ds(2 * q, 2)].reshape(256, 128) for side in range(2)]
        return jnp.concatenate(sides, axis=1)

    return pair_of


def adjoint_spectrum(r):
    start_specs(r)
    spectra(r, 0, COLS // 2, record_pairs(r), r.forward_table, NT_DIMS)
    turn_rows(r, COLS // 2 - 1)
    wait_spectra(r)
    wait_specs(r)

    def step(w):
        ah, al = split(r.x[w][:, :SPAD])
        both = split(jnp.concatenate([r.sr[w], r.si[w]], axis=1))
        wide = dot(jnp.concatenate([ah, al], axis=0), both[0])
        p = wide[:ROWS2] + (wide[ROWS2:] + dot(ah, both[1]))
        r.y[w] = jnp.concatenate(
            [p[:COLS, :PD] + p[COLS:, PD:], p[COLS:, :PD] - p[:COLS, PD:]], axis=0
        )

    over_frequencies(r, step)


def adjoint_samples(r, first, last):
    @pl.loop(first, last)
    def _(q):
        wait_columns(r, q)
        res = to_samples(
            lambda part: jnp.concatenate(
                [r.xn[part * COLS + 2 * q], r.xn[part * COLS + 2 * q + 1]], axis=1
            ),
            r.inverse_table,
        )
        r.adj[2 * q] = res[:, :PD]
        r.adj[2 * q + 1] = res[:, PD:]


def weighted_table(r):
    table = r.forward_table
    high, low = split(dot3((table[:, 0:NT], table[:, 256 : 256 + NT]), split(r.prior[...])))
    r.weighted[...] = jnp.zeros_like(r.weighted)
    for i, piece in enumerate((high, low, high)):
        r.weighted[:, 256 * i : 256 * i + NT] = piece


def field_spectra(r, first, last):
    def pair_of(q):
        pair = jnp.concatenate([r.all_adj[2 * q], r.all_adj[2 * q + 1]], axis=1)
        return jnp.concatenate([pair, jnp.zeros((256 - NT, 256), F32)], axis=0)

    spectra(r, first, last, pair_of, r.weighted, ((1,), (0,)))
    turn_rows(r, last - 1)


def predicted_spectrum(r):
    wait_spectra(r)

    def step(w):
        f = r.x[w]
        re, im = f[:COLS], f[COLS:]
        fh, fl = split(f)
        left = jnp.concatenate(
            [jnp.concatenate([fh, fh], axis=1), jnp.concatenate([fl, jnp.zeros_like(fl)], axis=1)],
            axis=0,
        )
        prods = []
        for s in (r.sr, r.si):
            wide = dot(left, jnp.concatenate(split(s[w]), axis=1), NT_DIMS)
            prods.append(wide[:ROWS2] + wide[ROWS2:])
        p, q = prods
        r.y[w, :, 0:SPAD] = jnp.concatenate([p[:COLS] - q[COLS:], p[COLS:] + q[:COLS]], axis=0)

    over_frequencies(r, step)


def predicted_samples(r, g):
    for k in range(GROUP // 2):
        wait_columns(r, g * GROUP // 2 + k)
    res = to_samples(
        lambda part: jnp.concatenate(
            [r.xn[part * COLS + g * GROUP + k][:, :SPAD] for k in range(GROUP)], axis=1
        ),
        r.block_table,
    )
    r.p[g] = res.reshape(8, 2, SPADT, WIDE)


def selection(r):
    keys = r.pick.shape[1]

    @pl.loop(0, 8)
    def _(i):
        at = pl.ds(pl.multiple_of(i * SPAD, SPAD), SPAD)
        row = lax.broadcasted_iota(jnp.int32, (SPAD, keys), 0)
        chosen = (row + i * SD == r.place[...]) & (row < SD)
        r.pick[at, :] = chosen.astype(F32).astype(BF16)


def split_inverse(r):
    @pl.loop(0, STEPS)
    def _(t):
        high, low = split(r.inv[t])
        r.ih[t] = high
        r.il[t] = low


def put_in_order(r, g):
    left = jnp.concatenate(
        [
            jnp.concatenate([r.gath[g, i][:, k * SPAD : (k + 1) * SPAD] for i in range(8)], axis=1)
            for k in range(GROUP)
        ],
        axis=0,
    )
    high, low = split(left)
    res = dot(high, r.pick[...]) + dot(low, r.pick[...])
    for k in range(GROUP):
        r.perm[:, g * GROUP + k, :] = res[k * SPADT : (k + 1) * SPADT, :]


def apply_inverse(r):
    rows = r.ih.shape[1]
    r.u[...] = jnp.zeros_like(r.u)

    @pl.loop(0, STEPS)
    def _(t):
        r.u[:, 0:rows] += dot3(split(r.perm[t]), (r.ih[t], r.il[t]), NT_DIMS)


def sum_all(r, send, half, place, up, down, over):
    x, y_hi = place
    start = half * HALF_ROWS
    start_b = start + 8 * HALF_A
    size_b = 8 * QUARTER_B
    a, out = r.adj_rows, r.all_rows
    swap_a, swap_b, half_b, done_a = (
        ref.at[half] for ref in (r.swap_a, r.swap_b, r.half_b, r.done_a)
    )

    def at_a(q, h):
        return rows_at(start + (2 * q + h) * HALF_A, HALF_A)

    def at_half_b(q, h):
        return rows_at((2 * q + h) * QUARTER_B, QUARTER_B)

    def place_b(q, h):
        return rows_at(start_b + y_hi * size_b + (2 * q + h) * QUARTER_B, QUARTER_B)

    theirs = rows_at(start_b + (1 - y_hi) * size_b, size_b)
    ours = rows_at(start_b + y_hi * size_b, size_b)
    to_over_b = send(a.at[theirs], swap_b, over)
    ring_a = RingSum(send, a, at_a, x, up, down, r.relay_a.at[half], r.arrive_a.at[half])
    yield
    ring_a.pass_on()
    to_over_b.wait_recv()
    half_b[...] = a[ours] + swap_b[...]
    ring_b = RingSum(send, half_b, at_half_b, x, up, down, r.relay_b.at[half], r.arrive_b.at[half])
    yield
    for h in range(2):
        done_a[h] = ring_a.half(h)
    to_over_a = send(done_a.at[1 - y_hi], swap_a, over)
    ring_b.pass_on()
    yield
    to_over_a.wait_recv()
    mine = at_a(x, y_hi)
    out[mine] = done_a[y_hi] + swap_a[...]
    back_a = send(out.at[mine], out.at[mine], over)
    for h in range(2):
        out[place_b(x, h)] = ring_b.half(h)
    spread_b = RingSpread(send, out, place_b, x, up, down)
    yield
    back_a.wait_recv()
    spread_a = RingSpread(send, out, at_a, x, up, down)
    spread_b.pass_on()
    yield
    spread_b.finish()
    back_b = send(out.at[ours], out.at[ours], over)
    spread_a.pass_on()
    yield
    spread_a.finish()
    back_b.wait_recv()
    yield


def sum_times(r, send, g, place, links):
    x, y_hi, y_lo, z, core = place
    next_z, last_z, beside, partner = links[:4]
    p, core_in, mine, own, swap, out = (
        ref.at[g] for ref in (r.p, r.core_in, r.mine, r.own, r.swap_t, r.gath)
    )
    order = [(h, (z + d) % 4) for d, h in ((2, 0), (2, 1), (1, 1), (3, 0), (1, 0), (3, 1), (0, 0), (0, 1))]
    swaps = [send(p.at[4 * h + q, 1 - core], core_in.at[4 * h + q], partner) for h, q in order]
    yield
    for copy, (h, q) in zip(swaps, order):
        m = 4 * h + q
        copy.wait_recv()
        mine[m] = p[m, core] + core_in[m]
    ring = RingSum(
        send, mine, lambda q, h: 4 * h + q, z, next_z, last_z, r.relay_t.at[g], r.arrive_t.at[g]
    )
    yield
    ring.pass_on()
    yield
    for h in range(2):
        own[h] = ring.half(h)
    to_beside = send(own.at[1 - y_lo], swap, beside)
    yield
    to_beside.wait_recv()
    sens = 2 * x + y_hi
    out[sens] = own[y_lo] + swap[...]

    copies = [send(out.at[sens], out.at[sens], to) for to in links[4:]]
    yield
    for copy in copies:
        copy.wait_recv()
    yield


def finish(r, send, others, sens, me):
    for c in range(COLS):
        r.rows[c] = jnp.broadcast_to(r.u[c : c + 1, :], (8, 128))
    sent = [send(r.rows.at[j], r.recv.at[d], (sens, j)) for d, j in enumerate(others)]
    total = r.rows[me]
    for d, copy in enumerate(sent):
        copy.wait_recv()
        total = total + r.recv[d]
    r.out[...] = total[0:1, 0 : r.out.shape[1]]


INPUTS = [
    "rec_in",
    "sr_hbm",
    "si_hbm",
    "prior",
    "place",
    "inv_hbm",
    "forward_table",
    "inverse_table",
    "block_table",
]
OUTPUTS = ["out", "rows_hbm", "freq_hbm"]


def scratch(keys, rows):
    dma = pltpu.SemaphoreType.DMA
    part = (HALVES,)
    t_block = (SPADT, WIDE)
    messages = 150
    return dict(
        sr=pltpu.VMEM((NF, SPAD, PD), F32),
        si=pltpu.VMEM((NF, SPAD, PD), F32),
        x=pltpu.VMEM((NF, ROWS2, 128), F32),
        y=pltpu.VMEM((NF, ROWS2, 128), F32),
        xn=pltpu.VMEM((ROWS2, 256, 128), F32),
        flat=pltpu.VMEM((2, SD, COLS, 128), F32),
        rec=pltpu.VMEM((2, COLS, 128, 128), F32),
        adj=pltpu.VMEM((COLS, NT, PD), F32),
        all_adj=pltpu.VMEM((COLS, NT, PD), F32),
        weighted=pltpu.VMEM((2 * FR, 768), BF16),
        relay_a=pltpu.VMEM((*part, 2, HALF_A, 128), F32),
        arrive_a=pltpu.VMEM((*part, 4, HALF_A, 128), F32),
        swap_a=pltpu.VMEM((*part, HALF_A, 128), F32),
        done_a=pltpu.VMEM((*part, 2, HALF_A, 128), F32),
        relay_b=pltpu.VMEM((*part, 2, QUARTER_B, 128), F32),
        arrive_b=pltpu.VMEM((*part, 4, QUARTER_B, 128), F32),
        swap_b=pltpu.VMEM((*part, 8 * QUARTER_B, 128), F32),
        half_b=pltpu.VMEM((*part, 8 * QUARTER_B, 128), F32),
        p=pltpu.VMEM((*part, 8, 2, *t_block), F32),
        core_in=pltpu.VMEM((*part, 8, *t_block), F32),
        mine=pltpu.VMEM((*part, 8, *t_block), F32),
        relay_t=pltpu.VMEM((*part, 2, *t_block), F32),
        arrive_t=pltpu.VMEM((*part, 4, *t_block), F32),
        own=pltpu.VMEM((*part, 2, *t_block), F32),
        swap_t=pltpu.VMEM((*part, *t_block), F32),
        gath=pltpu.VMEM((*part, 8, *t_block), F32),
        pick=pltpu.VMEM((8 * SPAD, keys), BF16),
        inv=pltpu.VMEM((STEPS, rows, keys), F32),
        ih=pltpu.VMEM((STEPS, rows, keys), BF16),
        il=pltpu.VMEM((STEPS, rows, keys), BF16),
        perm=pltpu.VMEM((SPADT, COLS, keys), F32),
        u=pltpu.VMEM((COLS, 128), F32),
        rows=pltpu.VMEM((COLS, 8, 128), F32),
        recv=pltpu.VMEM((COLS - 1, 8, 128), F32),
        spec_sem=dma((2,)),
        rsem=dma((2,)),
        xsem=dma((2, COLS // 2)),
        ysem=dma((NCHUNK,)),
        csem=dma((COLS // 2,)),
        inv_sem=dma,
        ssem=dma((messages,)),
        msem=dma((messages,)),
    )


def kernel(names, *refs):
    r = Refs(names, refs)
    r.adj_rows = r.adj.reshape(COLS * NT, PD)
    r.all_rows = r.all_adj.reshape(COLS * NT, PD)
    x, y_hi, y_lo, z, core = place = here()
    sens, me = lax.axis_index("sens"), lax.axis_index("par")
    up = device((x + 1) % 4, y_hi, y_lo, z, core)
    down = device((x + 3) % 4, y_hi, y_lo, z, core)
    over = device(x, 1 - y_hi, y_lo, z, core)
    next_z = device(x, y_hi, y_lo, (z + 1) % 4, core)
    last_z = device(x, y_hi, y_lo, (z + 3) % 4, core)
    beside = device(x, y_hi, 1 - y_lo, z, core)
    partner = device(x, y_hi, y_lo, z, 1 - core)
    others = [(me + d) % COLS for d in range(1, COLS)]
    friends = [(sens, j) for j in others]
    around = [device((x + d) % 4, (y_hi + e) % 2, y_lo, z, core) for e, d in PEERS]
    friends += around
    links = (next_z, last_z, beside, partner, *around)
    greet(friends)
    send = Sender(r.ssem, r.msem)
    adjoint_spectrum(r)
    inverse = pltpu.make_async_copy(r.inv_hbm, r.inv, r.inv_sem)
    inverse.start()
    pairs = COLS // 2 // HALVES
    adjoint_samples(r, 0, pairs)
    all_here(friends)
    first = sum_all(r, send, 0, (x, y_hi), up, down, over)
    next(first)
    adjoint_samples(r, pairs, 2 * pairs)
    second = sum_all(r, send, 1, (x, y_hi), up, down, over)
    next(second)
    weighted_table(r)
    for _ in range(4):
        next(first)
        next(second)
    selection(r)
    next(first)
    next(second)
    next(first)
    field_spectra(r, 0, pairs)
    next(second)
    field_spectra(r, pairs, 2 * pairs)
    predicted_spectrum(r)
    predicted_samples(r, 0)
    first = sum_times(r, send, 0, place, links)
    next(first)
    predicted_samples(r, 1)
    second = sum_times(r, send, 1, place, links)
    next(second)
    inverse.wait()
    for step in range(3):
        next(first)
        next(second)
    split_inverse(r)
    for step in range(1):
        next(first)
        next(second)
    next(first)
    put_in_order(r, 0)
    next(second)
    put_in_order(r, 1)
    apply_inverse(r)
    finish(r, send, others, sens, me)
    send.finish()


def shards(records, spec_real, spec_imag, prior_cov, sensor_map, inverse_rows):
    tabs = tables()
    sr, si = spec_real.transpose(1, 0, 2), spec_imag.transpose(1, 0, 2)
    place = sensor_map[None]
    rows, _, keys = inverse_rows.shape
    spaces = scratch(keys, rows)
    out, _, _ = pl.pallas_call(
        functools.partial(kernel, INPUTS + OUTPUTS + list(spaces)),
        out_shape=(
            jax.ShapeDtypeStruct((1, rows), F32),
            jax.ShapeDtypeStruct((ROWS2, NF, 128), F32),
            jax.ShapeDtypeStruct((NF, ROWS2, 128), F32),
        ),
        in_specs=[VMEM, ANY, ANY, VMEM, VMEM, ANY] + [VMEM] * 3,
        out_specs=(VMEM, HBM, HBM),
        scratch_shapes=list(spaces.values()),
        compiler_params=pltpu.CompilerParams(
            vmem_limit_bytes=LIMIT, collective_id=0, has_side_effects=True
        ),
        name="tsunami",
    )(records.transpose(1, 0, 2), sr, si, prior_cov, place, inverse_rows.transpose(1, 0, 2), *tabs)
    return out


def solution(mesh):
    return jax.shard_map(
        shards,
        mesh=mesh,
        in_specs=(
            P(None, "sens", None),
            P(None, "sens", "par"),
            P(None, "sens", "par"),
            P(),
            P(),
            P("sens", "par", None),
        ),
        out_specs=P("par", "sens"),
        check_vma=False,
    )
```

time: 367 us -> 109 us (0.30); the launches traced: 362 us -> 109 us
  matrix products: 151 us -> 0 us
  waiting for transfers between devices: 116 us -> 0 us
  Pallas kernels: 0 us -> 107 us
  local copies, waits for them, and re-layouts: 47.9 us -> 2.43 us
  starting transfers between devices: 18.1 us -> 0 us
  between operations: 13.8 us -> 0.01 us
  blocking collectives: 10.1 us -> 0 us
  other arithmetic: 5.21 us -> 0 us
    dot_general x19 -> x0, matrix products: 151 us -> none  [the longest x1 19.5 us: shards(): jnp.einsum('cpw,wsp->csw', field_imag, spec_imag, precision=highest, pref...]
    pallas_call x0 -> x1, Pallas kernels: none -> 107 us  [shards(): pl.pallas_call(functools.partial(kernel, INPUTS + OUTPUTS + list(spaces))...]
    all_gather x1 -> x0, waiting for transfers between devices: 67 us -> none  [side_by_side(): lax.all_gather(both, axis, axis=dim, tiled=True)]
    all_to_all x3 -> x0, waiting for transfers between devices: 48.6 us -> none  [the longest x2 37.8 us: sum_at_owner(): lax.all_to_all(pieces, axis, split_axis=0, concat_axis=0, tiled=True)]
    gather x2 -> x0, local copies, waits for them, and re-layouts: 22.2 us -> none  [shards(): permuted = jnp.take(gathered, pick_index, axis=1)]
    all_to_all x3 -> x0, starting transfers between devices: 17.7 us -> none  [the longest x2 13.3 us: sum_at_owner(): lax.all_to_all(pieces, axis, split_axis=0, concat_axis=0, tiled=True)]
    all_to_all x1 -> x0, blocking collectives: 10.1 us -> none  [sum_at_owner(): lax.all_to_all(pieces, axis, split_axis=0, concat_axis=0, tiled=True)]
    dot_general x2 -> x0, local copies, waits for them, and re-layouts: 5.9 us -> none  [the longest x1 3.09 us: to_spectrum(): jnp.dot(signal, cosine, precision=highest, preferred_element_type=jnp.flo...]
  transfers between devices with their start and end apart: 4 -> 0, of which waited for: 4 -> 0; matrix products, arithmetic and copies ran while one was open for 2% -> 0% of each run, Pallas kernels for 0% -> 0%
where the time goes in v2:
time: 109 us
  Pallas kernels  107 us (98%)
  local copies, waits for them, and re-layouts  2.43 us (2%)
    pallas_call x1, Pallas kernels, shards(): pl.pallas_call(functools.partial(kernel, INPUTS + OUTPUTS + list(spaces))...  107 us

profile of v2, /device:TPU:1, one launch (start us, length us, event | category | flops | bytes accessed | tf_op | source)
XLA Modules:
  0.0 109.1 jit_solution(5149896630067370258)
XLA Ops:
  0.0 1.3 %broadcast_in_dim.3.refs_4_ = s32[1,600]{1,0:T(1,128)} reshape(s32[600]{0:T(1024)} %param.13) | data formatting | bytes 4800 | tf_op jit(solution)/shard_map/broadcast_in_dim | solution.py:690
  1.3 106.6 %tsunami.1 = (f32[1,96]{1,0:T(1,128)}, f32[32,225,128]{2,1,0:T(8,128)}, f32[225,32,128]{2,1,0:T(8,128)}) custom-call(f32[75,16,224]{2,1,0:T(8,128)} %bitcast.7, f32[75,225,128]{2,1,0:T(8,128)} %bitcast.4, f32[75,225,128]{2,1,0:T(8,128)} %bitcast.5, f32[224,224]{1,0:T(8,128)} %refs_3_.1, s32[1,600]{1,0:T(1,128)} %broadcast_in_dim.3.refs_4_, ...), custom_call_target="tpu_custom_call" | custom-call | tf_op jit(solution)/shard_map/tsunami/pallas_call | solution.py:693
  107.9 1.1 %copy.11 = f32[1,96]{1,0:T(1,128)} copy(f32[1,96]{1,0:T(1,128)} %get-tuple-element.6) | data formatting | bytes 768

commit v3 on v2

--- a/solution.py
+++ b/solution.py
@@ -413,12 +413,13 @@
 
 def selection(r):
     keys = r.pick.shape[1]
+    where = r.place[...].reshape(1, keys)
 
     @pl.loop(0, 8)
     def _(i):
         at = pl.ds(pl.multiple_of(i * SPAD, SPAD), SPAD)
         row = lax.broadcasted_iota(jnp.int32, (SPAD, keys), 0)
-        chosen = (row + i * SD == r.place[...]) & (row < SD)
+        chosen = (row + i * SD == where) & (row < SD)
         r.pick[at, :] = chosen.astype(F32).astype(BF16)
 
 
@@ -641,6 +642,7 @@
     adjoint_spectrum(r)
     inverse = pltpu.make_async_copy(r.inv_hbm, r.inv, r.inv_sem)
     inverse.start()
+    weighted_table(r)
     pairs = COLS // 2 // HALVES
     adjoint_samples(r, 0, pairs)
     all_here(friends)
@@ -649,17 +651,18 @@
     adjoint_samples(r, pairs, 2 * pairs)
     second = sum_all(r, send, 1, (x, y_hi), up, down, over)
     next(second)
-    weighted_table(r)
     for _ in range(4):
         next(first)
         next(second)
-    selection(r)
     next(first)
     next(second)
     next(first)
     field_spectra(r, 0, pairs)
     next(second)
     field_spectra(r, pairs, 2 * pairs)
+    inverse.wait()
+    split_inverse(r)
+    selection(r)
     predicted_spectrum(r)
     predicted_samples(r, 0)
     first = sum_times(r, send, 0, place, links)
@@ -667,11 +670,9 @@
     predicted_samples(r, 1)
     second = sum_times(r, send, 1, place, links)
     next(second)
-    inverse.wait()
     for step in range(3):
         next(first)
         next(second)
-    split_inverse(r)
     for step in range(1):
         next(first)
         next(second)
@@ -687,7 +688,6 @@
 def shards(records, spec_real, spec_imag, prior_cov, sensor_map, inverse_rows):
     tabs = tables()
     sr, si = spec_real.transpose(1, 0, 2), spec_imag.transpose(1, 0, 2)
-    place = sensor_map[None]
     rows, _, keys = inverse_rows.shape
     spaces = scratch(keys, rows)
     out, _, _ = pl.pallas_call(
@@ -704,7 +704,7 @@
             vmem_limit_bytes=LIMIT, collective_id=0, has_side_effects=True
         ),
         name="tsunami",
-    )(records.transpose(1, 0, 2), sr, si, prior_cov, place, inverse_rows.transpose(1, 0, 2), *tabs)
+    )(records.transpose(1, 0, 2), sr, si, prior_cov, sensor_map, inverse_rows.transpose(1, 0, 2), *tabs)
     return out
 
 

time: 109 us -> 108 us (level)
  local copies, waits for them, and re-layouts: 2.43 us -> 1.17 us
    broadcast_in_dim x1 -> x0, local copies, waits for them, and re-layouts: 1.28 us -> none  [shards(): place = sensor_map[None]]
where the time goes in v3:
time: 108 us; the launch traced here: 107 us
  Pallas kernels  106 us (98%)
  local copies, waits for them, and re-layouts  1.17 us (1%)
    pallas_call x1, Pallas kernels, shards(): pl.pallas_call(functools.partial(kernel, INPUTS + OUTPUTS + list(spaces))...  106 us

profile of v3, /device:TPU:1, one launch (start us, length us, event | category | flops | bytes accessed | tf_op | source)
XLA Modules:
  0.0 107.4 jit_solution(18193586251777742596)
XLA Ops:
  0.0 106.2 %tsunami.1 = (f32[1,96]{1,0:T(1,128)}, f32[32,225,128]{2,1,0:T(8,128)}, f32[225,32,128]{2,1,0:T(8,128)}) custom-call(f32[75,16,224]{2,1,0:T(8,128)} %bitcast.7, f32[75,225,128]{2,1,0:T(8,128)} %bitcast.4, f32[75,225,128]{2,1,0:T(8,128)} %bitcast.5, f32[224,224]{1,0:T(8,128)} %refs_3_.1, s32[600]{0:T(1024)} %refs_4_.1, f32[14,96,600]{2,1,0:T(8,128)} %bitcast.6, ...), custom_call_target="tpu_custom_call" | custom-call | tf_op jit(solution)/shard_map/tsunami/pallas_call | solution.py:693
  106.2 1.2 %copy.11 = f32[1,96]{1,0:T(1,128)} copy(f32[1,96]{1,0:T(1,128)} %get-tuple-element.6) | data formatting | bytes 768
